TPU v7x, 32 devices: a whole 2x2x4 slice. The times are simulated.
32 devices in a mesh: rows: 8 (over z, y), cols: 4 (over x, core).
Axes of the slice: x: 2, y: 2, z: 4, core: 2. Of those that a mesh axis runs over, the one named last changes fastest.
Arguments:
- sketches: bfloat16 [2048, 16384], P('rows', 'cols'), may hold values from -6 to 6, as said below
- start_basis: bfloat16 [16384, 256], P('cols'), may hold values from -6 to 6
- shrink_index: int32 [1], replicated, may hold values from 64 to 191
Outputs:
- shrunk: float32 [256, 16384], P('rows', 'cols')
Inputs may be any that keep to these rules, and one draw needn't show every extreme that they name: `sketches`: real entries.
All inputs are finite; a program needn't handle non-finite values.
Results may differ from a plain program's by a relative error of at most 0.0028.
Values may be sent and summed in bfloat16 or wider, within the bound.
A program may use at most 64 MiB of HBM per device.

v0:
```python
import jax
import jax.numpy as jnp
from jax import lax
from jax.sharding import PartitionSpec as P

ITERS = 3


def project(sketches, basis_bf):
    partial_product = jnp.dot(sketches, basis_bf, preferred_element_type=jnp.float32)
    return lax.psum(partial_product, "cols")


def orthonormal(images, gram_total):
    lower_factor = jnp.linalg.cholesky(gram_total)
    return jax.scipy.linalg.solve_triangular(lower_factor, images.T, lower=True).T


def body(sketches, start_basis, shrink_index):
    basis_bf = start_basis
    basis = start_basis.astype(jnp.float32)
    for loop_index in range(ITERS):
        projected_bf = project(sketches, basis_bf).astype(jnp.bfloat16)
        local_images = jnp.einsum(
            "lw,lk->wk", sketches, projected_bf, preferred_element_type=jnp.float32
        )
        images = lax.psum(local_images, "rows")
        gram_total = lax.psum(jnp.dot(images.T, images, precision=lax.Precision.HIGHEST), "cols")
        basis = orthonormal(images, gram_total)
        basis_bf = basis.astype(jnp.bfloat16)
    projected = project(sketches, basis_bf)
    energy = lax.psum(jnp.sum(projected * projected, axis=0), "rows")
    ordered = jnp.sort(energy)[::-1]
    threshold = lax.dynamic_index_in_dim(ordered, shrink_index[0], 0, keepdims=False)
    factor = jnp.sqrt(jnp.maximum(energy - threshold, 0.25 * threshold))
    owned_rows = basis.shape[1] // lax.axis_size("rows")
    offset = lax.axis_index("rows") * owned_rows
    columns = lax.dynamic_slice_in_dim(basis, offset, owned_rows, 1)
    scaled = columns * lax.dynamic_slice_in_dim(factor, offset, owned_rows, 0)[None, :]
    return scaled.T


def solution(mesh):
    return jax.shard_map(
        body,
        mesh=mesh,
        in_specs=(P("rows", "cols"), P("cols", None), P()),
        out_specs=P("rows", "cols"),
        check_vma=False,
    )
```

profile of v0, /device:TPU:0, one launch (start us, length us, event | category | flops | bytes accessed | tf_op | source)
XLA Modules:
  0.0 932.8 jit_solution(5308531713813557644)
XLA Ops:
  6.5 1.6 copy-done
  8.1 2.3 fusion.53
  10.4 16.3 %all-reduce.25 = bf16[256,256]{1,0:T(8,128)(2,1)S(1)} all-reduce(f32[256,256]{1,0:T(8,128)S(1)} %fusion.53), channel_id=1, replica_groups=mesh['rows'=8,'cols'=4] {'cols'}, use_global_device_ids=true, to_apply=%region_0.0 | all-reduce | flops 65536 | bytes 393216 | tf_op jit(solution)/shard_map/psum | solution.py:11
  26.7 2.7 convolution_bitcast_fusion.2
  29.5 157.0 %all-reduce.12.cloned.1.call-done = f32[4096,256]{0,1:T(8,128)} async-done(((f32[4096,256]{0,1:T(8,128)}), f32[4096,256]{0,1:T(8,128)}) %all-reduce.12.cloned.1.call-update) | async-done | bytes 4194320 | tf_op jit(solution)/shard_map/psum | solution.py:27
  186.5 7.7 fusion.54
  194.7 30.9 %all-reduce.14.cloned.1.call-done = f32[256,256]{0,1:T(8,128)} async-done(((f32[256,256]{0,1:T(8,128)}), f32[256,256]{0,1:T(8,128)}) %all-reduce.14.cloned.1.call-update) | async-done | bytes 262160 | tf_op jit(solution)/shard_map/psum | solution.py:28
  227.7 11.7 %cholesky.172 = f32[128,128]{1,0:T(8,128)S(1)} custom-call(f32[128,128]{1,0:T(8,128)S(1)} %cholesky.270), custom_call_target="Cholesky" | custom-call | tf_op jit(solution)/shard_map/jit(cholesky)/cholesky | solution.py:15
  239.5 9.8 %custom-call.15 = f32[1,128,128]{1,2,0:T(8,128)S(1)} custom-call(f32[1,128,128]{2,1,0:T(8,128)S(1)} %get-tuple-element.74), custom_call_target="InvertDiagBlocksLowerTriangular" | custom-call | tf_op jit(solution)/shard_map/jit(cholesky)/cholesky | solution.py:15
  249.8 11.7 %cholesky.189 = f32[128,128]{1,0:T(8,128)S(1)} custom-call(f32[128,128]{1,0:T(8,128)S(1)} %convolution_subtract_fusion.5), custom_call_target="Cholesky" | custom-call | tf_op jit(solution)/shard_map/jit(cholesky)/cholesky | solution.py:15
  263.6 4.1 while.6
  264.4 1.4 bitcast_dynamic-update-slice_fusion.6
  266.3 1.4 bitcast_dynamic-update-slice_fusion.6
  267.7 19.7 %custom-call.16 = f32[2,128,128]{1,2,0:T(8,128)S(1)} custom-call(f32[2,128,128]{2,1,0:T(8,128)S(1)} %get-tuple-element.30), custom_call_target="InvertDiagBlocksLowerTriangular" | custom-call | tf_op jit(solution)/shard_map/jit(_solve_triangular)/triangular_solve | solution.py:16
  287.4 3.6 fusion.9
  291.1 2.0 convolution_subtract_fusion.2
  293.1 1.9 fusion.33
  295.9 13.5 %all-reduce.26 = bf16[256,256]{0,1:T(8,128)(2,1)S(1)} all-reduce(f32[256,256]{0,1:T(8,128)S(1)} %fusion.14), channel_id=1, replica_groups=mesh['rows'=8,'cols'=4] {'cols'}, use_global_device_ids=true, to_apply=%region_7.0 | all-reduce | flops 65536 | bytes 393216 | tf_op jit(solution)/shard_map/psum | solution.py:11
  309.4 2.7 convolution_bitcast_fusion.1
  312.1 156.6 %all-reduce.16.cloned.1.call-done = f32[4096,256]{0,1:T(8,128)} async-done(((f32[4096,256]{0,1:T(8,128)}), f32[4096,256]{0,1:T(8,128)}) %all-reduce.16.cloned.1.call-update) | async-done | bytes 4194320 | tf_op jit(solution)/shard_map/psum | solution.py:27
  468.7 7.7 fusion.55
  476.9 31.0 %all-reduce.18.cloned.1.call-done = f32[256,256]{0,1:T(8,128)} async-done(((f32[256,256]{0,1:T(8,128)}), f32[256,256]{0,1:T(8,128)}) %all-reduce.18.cloned.1.call-update) | async-done | bytes 262160 | tf_op jit(solution)/shard_map/psum | solution.py:28
  509.9 11.7 %cholesky.206 = f32[128,128]{1,0:T(8,128)S(1)} custom-call(f32[128,128]{1,0:T(8,128)S(1)} %cholesky.273), custom_call_target="Cholesky" | custom-call | tf_op jit(solution)/shard_map/jit(cholesky)/cholesky | solution.py:15
  521.7 9.8 %custom-call.17 = f32[1,128,128]{1,2,0:T(8,128)S(1)} custom-call(f32[1,128,128]{2,1,0:T(8,128)S(1)} %get-tuple-element.70), custom_call_target="InvertDiagBlocksLowerTriangular" | custom-call | tf_op jit(solution)/shard_map/jit(cholesky)/cholesky | solution.py:15
  532.0 11.7 %cholesky.223 = f32[128,128]{1,0:T(8,128)S(1)} custom-call(f32[128,128]{1,0:T(8,128)S(1)} %convolution_subtract_fusion.4), custom_call_target="Cholesky" | custom-call | tf_op jit(solution)/shard_map/jit(cholesky)/cholesky | solution.py:15
  546.4 4.1 while.7
  550.5 19.7 %custom-call.18 = f32[2,128,128]{1,2,0:T(8,128)S(1)} custom-call(f32[2,128,128]{2,1,0:T(8,128)S(1)} %get-tuple-element.31), custom_call_target="InvertDiagBlocksLowerTriangular" | custom-call | tf_op jit(solution)/shard_map/jit(_solve_triangular)/triangular_solve | solution.py:16
  570.2 3.6 fusion.7
  573.8 2.0 convolution_subtract_fusion.1
  575.8 1.9 fusion.29
  578.7 13.5 %all-reduce.27 = bf16[256,256]{0,1:T(8,128)(2,1)S(1)} all-reduce(f32[256,256]{0,1:T(8,128)S(1)} %fusion.15), channel_id=1, replica_groups=mesh['rows'=8,'cols'=4] {'cols'}, use_global_device_ids=true, to_apply=%region_10.0 | all-reduce | flops 65536 | bytes 393216 | tf_op jit(solution)/shard_map/psum | solution.py:11
  592.2 2.7 convolution_bitcast_fusion
  594.9 156.5 %all-reduce.20.cloned.1.call-done = f32[4096,256]{0,1:T(8,128)} async-done(((f32[4096,256]{0,1:T(8,128)}), f32[4096,256]{0,1:T(8,128)}) %all-reduce.20.cloned.1.call-update) | async-done | bytes 4194320 | tf_op jit(solution)/shard_map/psum | solution.py:27
  751.5 7.7 fusion.56
  759.4 31.2 %all-reduce.22.cloned.1.call-done = f32[256,256]{0,1:T(8,128)} async-done(((f32[256,256]{0,1:T(8,128)}), f32[256,256]{0,1:T(8,128)}) %all-reduce.22.cloned.1.call-update) | async-done | bytes 262160 | tf_op jit(solution)/shard_map/psum | solution.py:28
  792.7 11.7 %cholesky.240 = f32[128,128]{1,0:T(8,128)S(1)} custom-call(f32[128,128]{1,0:T(8,128)S(1)} %cholesky.276), custom_call_target="Cholesky" | custom-call | tf_op jit(solution)/shard_map/jit(cholesky)/cholesky | solution.py:15
  804.5 9.8 %custom-call.19 = f32[1,128,128]{1,2,0:T(8,128)S(1)} custom-call(f32[1,128,128]{2,1,0:T(8,128)S(1)} %get-tuple-element.66), custom_call_target="InvertDiagBlocksLowerTriangular" | custom-call | tf_op jit(solution)/shard_map/jit(cholesky)/cholesky | solution.py:15
  814.8 11.7 %cholesky.257 = f32[128,128]{1,0:T(8,128)S(1)} custom-call(f32[128,128]{1,0:T(8,128)S(1)} %convolution_subtract_fusion.3), custom_call_target="Cholesky" | custom-call | tf_op jit(solution)/shard_map/jit(cholesky)/cholesky | solution.py:15
  829.1 4.2 while.8
  833.3 19.7 %custom-call.20 = f32[2,128,128]{1,2,0:T(8,128)S(1)} custom-call(f32[2,128,128]{2,1,0:T(8,128)S(1)} %get-tuple-element.32), custom_call_target="InvertDiagBlocksLowerTriangular" | custom-call | tf_op jit(solution)/shard_map/jit(_solve_triangular)/triangular_solve | solution.py:16
  853.0 3.6 fusion.5
  856.7 1.9 convolution_subtract_fusion
  858.6 1.9 fusion.25
  861.9 1.5 fusion.11
  864.0 31.8 %all-reduce.24.cloned.1.call-done = f32[256,256]{0,1:T(8,128)} async-done(((f32[256,256]{0,1:T(8,128)}), f32[256,256]{0,1:T(8,128)}) %all-reduce.24.cloned.1.call-update) | async-done | bytes 262160 | tf_op jit(solution)/shard_map/psum | solution.py:11
  896.9 21.4 %psum.87 = f32[256]{0:T(256)S(1)} all-reduce(f32[256]{0:T(256)S(1)} %multiply_reduce_fusion), channel_id=1, replica_groups=mesh['rows'=8,'cols'=4] {'rows'}, use_global_device_ids=true, to_apply=%region_15.18 | all-reduce | flops 256 | bytes 2048 | tf_op jit(solution)/shard_map/psum | solution.py:32
  918.3 3.3 sort.15
  923.6 1.9 fusion.17
  (86 shorter events, 27.3 us)
Async XLA Ops:
  6.5 1.6 copy-start
  6.5 179.9 %all-reduce.12.cloned.1.call-start = ((), (), s32[]{:S(2)}) async-start(), calls=%async_computation | async-start | bytes 8388608 | tf_op jit(solution)/shard_map/psum | solution.py:27
  29.4 196.2 %all-reduce.14.cloned.1.call-start = ((), (), s32[]{:S(2)}) async-start(), calls=%async_computation.1 | async-start | bytes 524288 | tf_op jit(solution)/shard_map/psum | solution.py:28
  194.2 274.5 %all-reduce.16.cloned.1.call-start = ((), (), s32[]{:S(2)}) async-start(), calls=%async_computation.2 | async-start | bytes 8388608 | tf_op jit(solution)/shard_map/psum | solution.py:27
  287.4 3.7 copy-start.1
  312.1 195.8 %all-reduce.18.cloned.1.call-start = ((), (), s32[]{:S(2)}) async-start(), calls=%async_computation.3 | async-start | bytes 524288 | tf_op jit(solution)/shard_map/psum | solution.py:28
  476.4 275.0 %all-reduce.20.cloned.1.call-start = ((), (), s32[]{:S(2)}) async-start(), calls=%async_computation.4 | async-start | bytes 8388608 | tf_op jit(solution)/shard_map/psum | solution.py:27
  570.2 3.7 copy-start.3
  594.9 195.7 %all-reduce.22.cloned.1.call-start = ((), (), s32[]{:S(2)}) async-start(), calls=%async_computation.5 | async-start | bytes 524288 | tf_op jit(solution)/shard_map/psum | solution.py:28
  759.2 136.6 %all-reduce.24.cloned.1.call-start = ((), (), s32[]{:S(2)}) async-start(), calls=%async_computation.6 | async-start | bytes 524288 | tf_op jit(solution)/shard_map/psum | solution.py:11
  853.0 3.7 copy-start.2
  856.7 3.9 copy-start.4
  860.6 1.3 copy-start.5
Sparse Core Ops, SparseCore 0:
  29.6 156.8 all-reduce.11
  194.3 31.2 all-reduce.13
  312.2 156.4 all-reduce.15
  476.5 31.2 all-reduce.17
  595.0 156.4 all-reduce.19
  759.3 31.2 all-reduce.21
  863.5 32.2 all-reduce.23
where the time goes:
time: 938 us; the launch traced here: 933 us
  waiting for transfers between devices  595 us (63%)
  other arithmetic  172 us (18%)
  blocking collectives  64.6 us (7%)
  matrix products  60.7 us (6%)
  between operations  19.5 us (2%)
  local copies, waits for them, and re-layouts  18.7 us (2%)
    psum x3, waiting for transfers between devices, body(): images = lax.psum(local_images, 'rows')  470 us
    another operation x20, other arithmetic, orthonormal(): lower_factor = jnp.linalg.cholesky(gram_total)  103 us
    psum x3, waiting for transfers between devices, body(): lax.psum(jnp.dot(images.T, images, precision=lax.Precision.HIGHEST), 'cols')  93 us
    another operation x7, other arithmetic, orthonormal(): jax.scipy.linalg.solve_triangular(lower_factor, images.T, lower=True)  59.1 us
    psum x3, blocking collectives, project(): return lax.psum(partial_product, 'cols')  43.3 us
    psum x1, waiting for transfers between devices, project(): return lax.psum(partial_product, 'cols')  31.8 us
    dot_general x3, matrix products, body(): jnp.dot(images.T, images, precision=lax.Precision.HIGHEST)  23.1 us
    another operation x9, matrix products, orthonormal(): jax.scipy.linalg.solve_triangular(lower_factor, images.T, lower=True)  22.6 us
  transfers between devices with their start and end apart: 7, of which 7 were waited for; matrix products, arithmetic and copies ran while one was open for 0% of the time, Pallas kernels for 0%

commit v1 on v0

--- a/solution.py
+++ b/solution.py
@@ -24,7 +24,9 @@
         local_images = jnp.einsum(
             "lw,lk->wk", sketches, projected_bf, preferred_element_type=jnp.float32
         )
-        images = lax.psum(local_images, "rows")
+        images = local_images
+        for hop in (1, 2, 4):
+            images = images + lax.ppermute(images, "rows", [(dev, dev ^ hop) for dev in range(8)])
         gram_total = lax.psum(jnp.dot(images.T, images, precision=lax.Precision.HIGHEST), "cols")
         basis = orthonormal(images, gram_total)
         basis_bf = basis.astype(jnp.bfloat16)

time: 938 us -> 1580 us (1.68)
  waiting for transfers between devices: 595 us -> 1190 us
  other arithmetic: 172 us -> 200 us
  starting transfers between devices: 1.33 us -> 17.9 us
    ppermute x0 -> x9, waiting for transfers between devices: none -> 1070 us  [body(): lax.ppermute(images, 'rows', [(dev, dev ^ hop) for dev in range(8)])]
    psum x3 -> x0, waiting for transfers between devices: 470 us -> none  [body(): images = lax.psum(local_images, 'rows')]
    transpose x0 -> x3, other arithmetic: none -> 18.3 us  [body(): gram_total = lax.psum(jnp.dot(images.T, images, precision=lax.Precision.H...]
    ppermute x0 -> x9, starting transfers between devices: none -> 17.2 us  [body(): lax.ppermute(images, 'rows', [(dev, dev ^ hop) for dev in range(8)])]
  transfers between devices with their start and end apart: 7 -> 13, of which waited for: 7 -> 13; matrix products, arithmetic and copies ran while one was open for 0% -> 1% of each run, Pallas kernels for 0% -> 0%
where the time goes in v1:
time: 1580 us
  waiting for transfers between devices  1190 us (75%)
  other arithmetic  200 us (13%)
  blocking collectives  64.6 us (4%)
  matrix products  62.1 us (4%)
  local copies, waits for them, and re-layouts  20 us (1%)
  between operations  18.8 us (1%)
  starting transfers between devices  17.9 us (1%)
    ppermute x9, waiting for transfers between devices, body(): lax.ppermute(images, 'rows', [(dev, dev ^ hop) for dev in range(8)])  1070 us
    another operation x20, other arithmetic, orthonormal(): lower_factor = jnp.linalg.cholesky(gram_total)  103 us
    psum x3, waiting for transfers between devices, body(): lax.psum(jnp.dot(images.T, images, precision=lax.Precision.HIGHEST), 'cols')  92.4 us
    another operation x7, other arithmetic, orthonormal(): jax.scipy.linalg.solve_triangular(lower_factor, images.T, lower=True)  59.1 us
    psum x3, blocking collectives, project(): return lax.psum(partial_product, 'cols')  43.3 us
    psum x1, waiting for transfers between devices, project(): return lax.psum(partial_product, 'cols')  31.8 us
  transfers between devices with their start and end apart: 13, of which 13 were waited for; matrix products, arithmetic and copies ran while one was open for 1% of the time, Pallas kernels for 0%

profile of v1, /device:TPU:0, one launch (start us, length us, event | category | flops | bytes accessed | tf_op | source)
XLA Modules:
  0.0 1578.1 jit_solution(3236673249336293420)
XLA Ops:
  10.4 16.3 %all-reduce.16 = bf16[256,256]{1,0:T(8,128)(2,1)S(1)} all-reduce(f32[256,256]{1,0:T(8,128)S(1)} %fusion.62), channel_id=1, replica_groups=mesh['rows'=8,'cols'=4] {'cols'}, use_global_device_ids=true, to_apply=%region_0.0 | all-reduce | flops 65536 | bytes 393216 | tf_op jit(solution)/shard_map/psum | solution.py:11
  29.0 89.6 %collective-permute-done = f32[4096,256]{0,1:T(8,128)S(1)} collective-permute-done((f32[4096,256]{0,1:T(8,128)S(1)}, f32[4096,256]{0,1:T(8,128)S(1)}, u32[]{:S(2)}, u32[]{:S(2)}) %collective-permute-start) | collective-permute-done | bytes 4194336 | tf_op jit(solution)/shard_map/ppermute | solution.py:29
  121.1 88.7 %collective-permute-done.1 = f32[4096,256]{0,1:T(8,128)S(1)} collective-permute-done((f32[4096,256]{0,1:T(8,128)S(1)}, f32[4096,256]{0,1:T(8,128)S(1)}, u32[]{:S(2)}, u32[]{:S(2)}) %collective-permute-start.1) | collective-permute-done | bytes 4194336 | tf_op jit(solution)/shard_map/ppermute | solution.py:29
  209.8 2.5 add.70
  212.3 2.7 collective-permute-start.2
  215.0 178.0 %collective-permute-done.2 = f32[4096,256]{0,1:T(8,128)} collective-permute-done((f32[4096,256]{0,1:T(8,128)}, f32[4096,256]{0,1:T(8,128)}, u32[]{:S(2)}, u32[]{:S(2)}) %collective-permute-start.2) | collective-permute-done | bytes 4194336 | tf_op jit(solution)/shard_map/ppermute | solution.py:29
  393.0 10.4 fusion.18
  403.6 6.1 add_bitcast_fusion.2
  409.7 30.5 %all-reduce.9.cloned.1.call-done = f32[256,256]{0,1:T(8,128)} async-done(((f32[256,256]{0,1:T(8,128)}), f32[256,256]{0,1:T(8,128)}) %all-reduce.9.cloned.1.call-update) | async-done | bytes 262160 | tf_op jit(solution)/shard_map/psum | solution.py:30
  442.3 11.7 cholesky.172
  454.1 9.8 custom-call.15
  464.4 11.7 cholesky.189
  478.1 4.3 while.6
  482.4 19.7 %custom-call.16 = f32[2,128,128]{1,2,0:T(8,128)S(1)} custom-call(f32[2,128,128]{2,1,0:T(8,128)S(1)} %get-tuple-element.30), custom_call_target="InvertDiagBlocksLowerTriangular" | custom-call | tf_op jit(solution)/shard_map/jit(_solve_triangular)/triangular_solve | solution.py:16
  502.1 3.5 fusion.12
  510.5 13.5 all-reduce.17
  526.3 89.6 %collective-permute-done.3 = f32[4096,256]{0,1:T(8,128)S(1)} collective-permute-done((f32[4096,256]{0,1:T(8,128)S(1)}, f32[4096,256]{0,1:T(8,128)S(1)}, u32[]{:S(2)}, u32[]{:S(2)}) %collective-permute-start.3) | collective-permute-done | bytes 4194336 | tf_op jit(solution)/shard_map/ppermute | solution.py:29
  618.2 88.8 %collective-permute-done.4 = f32[4096,256]{0,1:T(8,128)S(1)} collective-permute-done((f32[4096,256]{0,1:T(8,128)S(1)}, f32[4096,256]{0,1:T(8,128)S(1)}, u32[]{:S(2)}, u32[]{:S(2)}) %collective-permute-start.4) | collective-permute-done | bytes 4194336 | tf_op jit(solution)/shard_map/ppermute | solution.py:29
  707.0 2.5 add.73
  709.5 2.4 collective-permute-start.5
  711.9 178.2 %collective-permute-done.5 = f32[4096,256]{0,1:T(8,128)} collective-permute-done((f32[4096,256]{0,1:T(8,128)}, f32[4096,256]{0,1:T(8,128)}, u32[]{:S(2)}, u32[]{:S(2)}) %collective-permute-start.5) | collective-permute-done | bytes 4194336 | tf_op jit(solution)/shard_map/ppermute | solution.py:29
  890.1 10.4 fusion.16
  900.7 6.1 add_bitcast_fusion.1
  906.8 31.0 %all-reduce.11.cloned.1.call-done = f32[256,256]{0,1:T(8,128)} async-done(((f32[256,256]{0,1:T(8,128)}), f32[256,256]{0,1:T(8,128)}) %all-reduce.11.cloned.1.call-update) | async-done | bytes 262160 | tf_op jit(solution)/shard_map/psum | solution.py:30
  939.8 11.7 cholesky.206
  951.6 9.8 custom-call.17
  961.9 11.7 cholesky.223
  976.2 4.3 while.7
  980.4 19.7 %custom-call.18 = f32[2,128,128]{1,2,0:T(8,128)S(1)} custom-call(f32[2,128,128]{2,1,0:T(8,128)S(1)} %get-tuple-element.31), custom_call_target="InvertDiagBlocksLowerTriangular" | custom-call | tf_op jit(solution)/shard_map/jit(_solve_triangular)/triangular_solve | solution.py:16
  1000.1 3.5 fusion.9
  1008.6 13.5 all-reduce.18
  1024.4 89.6 %collective-permute-done.6 = f32[4096,256]{0,1:T(8,128)S(1)} collective-permute-done((f32[4096,256]{0,1:T(8,128)S(1)}, f32[4096,256]{0,1:T(8,128)S(1)}, u32[]{:S(2)}, u32[]{:S(2)}) %collective-permute-start.6) | collective-permute-done | bytes 4194336 | tf_op jit(solution)/shard_map/ppermute | solution.py:29
  1116.2 88.8 %collective-permute-done.7 = f32[4096,256]{0,1:T(8,128)S(1)} collective-permute-done((f32[4096,256]{0,1:T(8,128)S(1)}, f32[4096,256]{0,1:T(8,128)S(1)}, u32[]{:S(2)}, u32[]{:S(2)}) %collective-permute-start.7) | collective-permute-done | bytes 4194336 | tf_op jit(solution)/shard_map/ppermute | solution.py:29
  1205.1 2.5 add.76
  1207.5 2.4 collective-permute-start.8
  1209.9 178.2 %collective-permute-done.8 = f32[4096,256]{0,1:T(8,128)} collective-permute-done((f32[4096,256]{0,1:T(8,128)}, f32[4096,256]{0,1:T(8,128)}, u32[]{:S(2)}, u32[]{:S(2)}) %collective-permute-start.8) | collective-permute-done | bytes 4194336 | tf_op jit(solution)/shard_map/ppermute | solution.py:29
  1388.1 10.4 fusion.14
  1398.7 6.1 add_bitcast_fusion
  1404.8 31.0 %all-reduce.13.cloned.1.call-done = f32[256,256]{0,1:T(8,128)} async-done(((f32[256,256]{0,1:T(8,128)}), f32[256,256]{0,1:T(8,128)}) %all-reduce.13.cloned.1.call-update) | async-done | bytes 262160 | tf_op jit(solution)/shard_map/psum | solution.py:30
  1437.9 11.7 cholesky.240
  1449.6 9.8 custom-call.19
  1459.9 11.7 cholesky.257
  1474.2 4.1 while.8
  1478.3 19.7 %custom-call.20 = f32[2,128,128]{1,2,0:T(8,128)S(1)} custom-call(f32[2,128,128]{2,1,0:T(8,128)S(1)} %get-tuple-element.32), custom_call_target="InvertDiagBlocksLowerTriangular" | custom-call | tf_op jit(solution)/shard_map/jit(_solve_triangular)/triangular_solve | solution.py:16
  1498.0 3.5 fusion.6
  1509.9 31.8 %all-reduce.15.cloned.1.call-done = f32[256,256]{0,1:T(8,128)} async-done(((f32[256,256]{0,1:T(8,128)}), f32[256,256]{0,1:T(8,128)}) %all-reduce.15.cloned.1.call-update) | async-done | bytes 262160 | tf_op jit(solution)/shard_map/psum | solution.py:11
  1542.7 21.4 %psum.63 = f32[256]{0:T(256)S(1)} all-reduce(f32[256]{0:T(256)S(1)} %multiply_reduce_fusion), channel_id=1, replica_groups=mesh['rows'=8,'cols'=4] {'rows'}, use_global_device_ids=true, to_apply=%region_12.15 | all-reduce | flops 256 | bytes 2048 | tf_op jit(solution)/shard_map/psum | solution.py:34
  1564.1 3.3 sort.15
  (104 shorter events, 63.0 us)
Async XLA Ops:
  6.5 1.6 copy-start
  6.5 433.7 %all-reduce.9.cloned.1.call-start = ((), (), s32[]{:S(2)}) async-start(), calls=%async_computation | async-start | bytes 524288 | tf_op jit(solution)/shard_map/psum | solution.py:30
  27.4 91.1 %collective-permute-start = (f32[4096,256]{0,1:T(8,128)S(1)}, f32[4096,256]{0,1:T(8,128)S(1)}, u32[]{:S(2)}, u32[]{:S(2)}) collective-permute-start(f32[4096,256]{0,1:T(8,128)S(1)} %convolution_bitcast_fusion.2), channel_id=1, source_target_pairs={{0,4},{4,0},{8,12},{12,8},{16,20},{20,16},{24,28},{28,24},{1,5},{5... | collective-permute-start | bytes 12582920 | tf_op jit(solution)/shard_map/ppermute | solution.py:29
  119.2 90.6 %collective-permute-start.1 = (f32[4096,256]{0,1:T(8,128)S(1)}, f32[4096,256]{0,1:T(8,128)S(1)}, u32[]{:S(2)}, u32[]{:S(2)}) collective-permute-start(f32[4096,256]{0,1:T(8,128)S(1)} %add.69), channel_id=1, source_target_pairs={{0,8},{4,12},{8,0},{12,4},{16,24},{20,28},{24,16},{28,20},{1,9},{5... | collective-permute-start | bytes 12582920 | tf_op jit(solution)/shard_map/ppermute | solution.py:29
  212.3 180.8 %collective-permute-start.2 = (f32[4096,256]{0,1:T(8,128)}, f32[4096,256]{0,1:T(8,128)}, u32[]{:S(2)}, u32[]{:S(2)}) collective-permute-start(f32[4096,256]{0,1:T(8,128)} %add.70), channel_id=1, source_target_pairs={{0,16},{4,20},{8,24},{12,28},{16,0},{20,4},{24,8},{28,12},{1,17},{... | collective-permute-start | bytes 12582920 | tf_op jit(solution)/shard_map/ppermute | solution.py:29
  403.4 534.3 %all-reduce.11.cloned.1.call-start = ((), (), s32[]{:S(2)}) async-start(), calls=%async_computation.1 | async-start | bytes 524288 | tf_op jit(solution)/shard_map/psum | solution.py:30
  505.6 2.2 copy-start.4
  524.7 91.2 %collective-permute-start.3 = (f32[4096,256]{0,1:T(8,128)S(1)}, f32[4096,256]{0,1:T(8,128)S(1)}, u32[]{:S(2)}, u32[]{:S(2)}) collective-permute-start(f32[4096,256]{0,1:T(8,128)S(1)} %convolution_bitcast_fusion.1), channel_id=1, source_target_pairs={{0,4},{4,0},{8,12},{12,8},{16,20},{20,16},{24,28},{28,24},{1,5},{5... | collective-permute-start | bytes 12582920 | tf_op jit(solution)/shard_map/ppermute | solution.py:29
  616.6 90.4 %collective-permute-start.4 = (f32[4096,256]{0,1:T(8,128)S(1)}, f32[4096,256]{0,1:T(8,128)S(1)}, u32[]{:S(2)}, u32[]{:S(2)}) collective-permute-start(f32[4096,256]{0,1:T(8,128)S(1)} %add.72), channel_id=1, source_target_pairs={{0,8},{4,12},{8,0},{12,4},{16,24},{20,28},{24,16},{28,20},{1,9},{5... | collective-permute-start | bytes 12582920 | tf_op jit(solution)/shard_map/ppermute | solution.py:29
  709.5 180.6 %collective-permute-start.5 = (f32[4096,256]{0,1:T(8,128)}, f32[4096,256]{0,1:T(8,128)}, u32[]{:S(2)}, u32[]{:S(2)}) collective-permute-start(f32[4096,256]{0,1:T(8,128)} %add.73), channel_id=1, source_target_pairs={{0,16},{4,20},{8,24},{12,28},{16,0},{20,4},{24,8},{28,12},{1,17},{... | collective-permute-start | bytes 12582920 | tf_op jit(solution)/shard_map/ppermute | solution.py:29
  900.5 535.3 %all-reduce.13.cloned.1.call-start = ((), (), s32[]{:S(2)}) async-start(), calls=%async_computation.2 | async-start | bytes 524288 | tf_op jit(solution)/shard_map/psum | solution.py:30
  1003.6 2.2 copy-start.5
  1022.8 91.2 %collective-permute-start.6 = (f32[4096,256]{0,1:T(8,128)S(1)}, f32[4096,256]{0,1:T(8,128)S(1)}, u32[]{:S(2)}, u32[]{:S(2)}) collective-permute-start(f32[4096,256]{0,1:T(8,128)S(1)} %convolution_bitcast_fusion), channel_id=1, source_target_pairs={{0,4},{4,0},{8,12},{12,8},{16,20},{20,16},{24,28},{28,24},{1,5},{5... | collective-permute-start | bytes 12582920 | tf_op jit(solution)/shard_map/ppermute | solution.py:29
  1114.7 90.4 %collective-permute-start.7 = (f32[4096,256]{0,1:T(8,128)S(1)}, f32[4096,256]{0,1:T(8,128)S(1)}, u32[]{:S(2)}, u32[]{:S(2)}) collective-permute-start(f32[4096,256]{0,1:T(8,128)S(1)} %add.75), channel_id=1, source_target_pairs={{0,8},{4,12},{8,0},{12,4},{16,24},{20,28},{24,16},{28,20},{1,9},{5... | collective-permute-start | bytes 12582920 | tf_op jit(solution)/shard_map/ppermute | solution.py:29
  1207.5 180.6 %collective-permute-start.8 = (f32[4096,256]{0,1:T(8,128)}, f32[4096,256]{0,1:T(8,128)}, u32[]{:S(2)}, u32[]{:S(2)}) collective-permute-start(f32[4096,256]{0,1:T(8,128)} %add.76), channel_id=1, source_target_pairs={{0,16},{4,20},{8,24},{12,28},{16,0},{20,4},{24,8},{28,12},{1,17},{... | collective-permute-start | bytes 12582920 | tf_op jit(solution)/shard_map/ppermute | solution.py:29
  1398.5 143.1 %all-reduce.15.cloned.1.call-start = ((), (), s32[]{:S(2)}) async-start(), calls=%async_computation.3 | async-start | bytes 524288 | tf_op jit(solution)/shard_map/psum | solution.py:11
  1501.5 4.9 copy-start.1
  1501.5 2.9 copy-start.3
  1506.4 1.3 copy-start.2
Sparse Core Ops, SparseCore 0:
  403.5 36.6 all-reduce.8
  900.6 37.1 all-reduce.10
  1398.6 37.1 all-reduce.12
  1509.3 32.2 all-reduce.14
